TPU v7x, 32 devices: a whole 2x2x4 slice. The times are simulated.
32 devices in a mesh: uv: 16 (over z, y, core), freq: 2 (over x).
Axes of the slice: x: 2, y: 2, z: 4, core: 2. Of those that a mesh axis runs over, the one named last changes fastest.
Arguments:
- visibility: float32 [2, 512, 8, 128], P('freq', 'uv'), may hold values from -6 to 6
- uv_offset: float32 [2, 512, 2, 128], P('freq', 'uv'), may hold values from -12 to 12
- w_offset: float32 [2, 512, 128], P('freq', 'uv'), may hold values from -40 to 40
- taper: float32 [32, 32], replicated, may hold values from 0.2 to 1
- row_count: int32 [2, 512], P('freq', 'uv'), may hold values from 1 to 128, as said below
- block_owner: int32 [2, 512, 1], P('freq', 'uv'), may hold values from 0 to 15; in each aligned block of 32 rows (0 to 31, 32 to 63, ..., all dimensions but the last counted through in order) at most 4 rows name the same one
- block_slot: int32 [2, 512], P('freq', 'uv'), may hold values from 0 to 15
- subgrid_offset: int32 [256, 2], P('uv'), may hold values from 0 to 96
Outputs:
- grid: float32 [2048, 8, 128], P(('uv', 'freq'))
Inputs may be any that keep to these rules, and one draw needn't show every extreme that they name: `block_owner`: among the 32 blocks of one device at most 4 name the same owner, a bound that some block reaches of them. `row_count`: some block has all 128 rows live.
All inputs are finite; a program needn't handle non-finite values.
Results may differ from a plain program's by a relative error of at most 0.0003.
Values sent between devices are 32-bit elements; how exact they have to be, the bound alone decides.
No kernel may reach another device: no remote copies, remote signals or barrier semaphores. Data moves between devices by JAX's collectives and lax.ppermute only.
A program may use at most 64 MiB of HBM per device.

v0:
```python
import functools
import math

import jax
import jax.numpy as jnp
import numpy as np
from jax import lax
from jax.experimental import pallas as pl
from jax.experimental.pallas import tpu as pltpu
from jax.sharding import PartitionSpec as P

TILE = 128
LANES = 128
COMPS = 8
field_width = 0.5

F32 = jnp.float32
BF16 = jnp.bfloat16


def fit_even(function, degree):
    points = np.cos(np.pi * (np.arange(400) + 0.5) / 400) * 0.125 + 0.125
    fit = np.polynomial.chebyshev.Chebyshev.fit(points, function(np.sqrt(points)), degree, domain=[0, 0.25])
    return [float(c) for c in fit.convert(kind=np.polynomial.Polynomial).coef]


SIN_COEF = fit_even(lambda f: math.sqrt(2) * np.sin(np.pi * f) / f, 3)
COS_COEF = fit_even(lambda f: math.sqrt(2) * np.cos(np.pi * f), 4)


def cos_sin_turns(turns):
    frac = turns - jnp.round(turns)
    square = frac * frac
    cos_half = COS_COEF[-1] * square + COS_COEF[-2]
    sin_half = SIN_COEF[-1] * square + SIN_COEF[-2]
    for c in COS_COEF[-3::-1]:
        cos_half = cos_half * square + c
    for c in SIN_COEF[-3::-1]:
        sin_half = sin_half * square + c
    sin_half = sin_half * frac
    return 1.0 - sin_half * sin_half, sin_half * cos_half


def split(x):
    high = x.astype(BF16)
    return high, (x - high.astype(F32)).astype(BF16)


def iota(shape, axis):
    return lax.broadcasted_iota(jnp.int32, shape, axis)


def pack_kernel(count_ref, owner_ref, slot_ref, vis_ref, uv_ref, w_ref, out_ref, used_ref, *, cap):
    owners = out_ref.shape[0]
    blk = vis_ref.shape[2]
    blocks = vis_ref.shape[0]
    extra = out_ref.shape[1] - cap
    shape = (8, blk)
    row, lane = iota(shape, 0), iota(shape, 1)

    def clear(o, carry):
        used_ref[o] = 0
        for t in range(extra):
            out_ref[o, cap + t] = jnp.zeros(shape, F32)
        return carry

    lax.fori_loop(0, owners, clear, 0)

    def place(j, carry):
        o = owner_ref[j]
        r = used_ref[o]
        used_ref[o] = r + 1
        count = count_ref[j]
        out_ref[o, r] = vis_ref[j]
        u, v, w = uv_ref[j, 0:1, :], uv_ref[j, 1:2, :], w_ref[pl.ds(j, 1), :]
        part = row % 4
        coords = jnp.where(part == 0, u, jnp.where(part == 1, v, w))
        t = cap + r // 2
        mine = (row // 4 == r % 2) & (part < 3)
        out_ref[o, t] = jnp.where(mine, coords, out_ref[o, t])
        meta = jnp.where(lane == 2 * r, count.astype(F32), slot_ref[j].astype(F32))
        here = (row == 3) & (lane // 2 == r)
        out_ref[o, cap] = jnp.where(here, meta, out_ref[o, cap])
        return carry

    lax.fori_loop(0, blocks, place, 0)


def pack(counts, owner, slot, vis, uv, w, owners, cap):
    extra = (cap + 1) // 2
    blk = vis.shape[2]
    smem = pl.BlockSpec(memory_space=pltpu.SMEM)
    vmem = pl.BlockSpec(memory_space=pltpu.VMEM)
    return pl.pallas_call(
        functools.partial(pack_kernel, cap=cap),
        out_shape=jax.ShapeDtypeStruct((owners, cap + extra, 8, blk), F32),
        in_specs=[smem] * 3 + [vmem] * 3,
        out_specs=vmem,
        scratch_shapes=[pltpu.SMEM((owners,), jnp.int32)],
        name="pack",
    )(counts, owner, slot, vis, uv, w)


def transform_constants(sub, blk):
    half = sub // 2
    scale = 1.0 / math.sqrt(blk) / sub
    k = np.arange(sub)
    plus = np.zeros((4, half, sub), np.complex128)
    minus = np.zeros((4, half, sub), np.complex128)
    for a in range(half):
        up = np.exp(-2j * np.pi * k * (half + a) / sub) * scale
        down = np.exp(-2j * np.pi * k * (half - a) / sub) * scale
        if a == 0:
            plus[0, 0], plus[1, 0] = up, -1j * up
            minus[2, 0], minus[3, 0] = -1j * scale, scale
        else:
            plus[:, a] = [up, -1j * up, -1j * up, -up]
            minus[:, a] = [down, -1j * down, 1j * down, down]
    both = np.stack([plus, minus]).reshape(2, 4 * half, sub)
    blank = np.zeros((2, 4 * half, LANES - sub))
    coef = np.concatenate([both.real, blank, both.imag, blank], 2).astype(np.float32)
    pick = np.zeros((2, 4, half, sub), np.float32)
    for a in range(half):
        pick[0, :, a, half + a] = 1
        pick[1, :, a, half - a if a else 0] = 1
    return coef, pick.reshape(2, 4 * half, sub)


def tables_kernel(taper_ref, coef_ref, pick_ref, high_ref, low_ref):
    sub = taper_ref.shape[0]
    dims = (((1,), (1,)), ((), ()))
    plus, minus = [
        lax.dot_general(pick_ref[i], taper_ref[...], dims, precision=lax.Precision.HIGHEST)
        for i in range(2)
    ]
    for y in range(sub):
        m = plus[:, y : y + 1] * coef_ref[0] + minus[:, y : y + 1] * coef_ref[1]
        high_ref[y], low_ref[y] = split(m)


def tables(taper, blk):
    sub = taper.shape[0]
    coef, pick = transform_constants(sub, blk)
    vmem = pl.BlockSpec(memory_space=pltpu.VMEM)
    shape = jax.ShapeDtypeStruct((sub, 2 * sub, 2 * LANES), BF16)
    return pl.pallas_call(
        tables_kernel,
        out_shape=[shape, shape],
        in_specs=[vmem] * 3,
        out_specs=[vmem] * 2,
        name="tables",
    )(taper, jnp.asarray(coef), jnp.asarray(pick))


def twiddle_sines(sub):
    return [math.sin(2 * math.pi * k / sub) for k in range(1, sub // 4 + 1)]


def fourier(values, times):
    count = len(values)
    if count == 1:
        return values
    even, odd = fourier(values[0::2], times), fourier(values[1::2], times)
    odd = [times(x, k, count) for k, x in enumerate(odd)]
    return [e + o for e, o in zip(even, odd)] + [e - o for e, o in zip(even, odd)]


def tile_kernel(
    offset_ref, part_ref, recv_hbm, high_ref, low_ref, *refs, cap, sub, parts, chunks
):
    outs, rest = refs[:parts], refs[parts:]
    (
        meta_ref, fill_ref, recv_ref, n_ref, buf_v, buf_c, b_ref, w_ref, x16_ref, sums_ref, z_ref,
        tile_ref, twiddle_ref, sems,
    ) = rest
    owners = recv_ref.shape[0]
    owned = offset_ref.shape[0]
    blk = recv_ref.shape[3]
    half = sub // 2
    shape = (8, blk)
    row, lane = iota(shape, 0), iota(shape, 1)
    assert half == 16
    meta_copy = pltpu.make_async_copy(recv_hbm.at[:, cap], meta_ref, sems.at[0])
    recv_copy = pltpu.make_async_copy(recv_hbm, recv_ref, sems.at[1])
    meta_copy.start()
    recv_copy.start()

    step = field_width / sub
    rowf = row.astype(F32)

    def n_of(y, x):
        s = (x * x + y * y) * (step * step)
        return s / (1.0 + jnp.sqrt(1.0 - s))

    for j in range(8):
        n_ref[j] = n_of(float(j), rowf + 8.0)
        shifted = jnp.where(row >= j, 0.0, 8.0)
        n_ref[8 + j] = n_of(float(j) + shifted, rowf + shifted)
    n_ref[16] = n_of(rowf + 8.0, rowf + 8.0)
    n_ref[17] = n_of(float(half), rowf)
    n_ref[18] = n_of(float(half), rowf + 8.0)
    s_corner = 2.0 * half * half * step * step
    n_corner = s_corner / (1.0 + math.sqrt(1.0 - s_corner))
    tile_ref[...] = jnp.zeros_like(tile_ref)
    sums_ref[...] = jnp.zeros_like(sums_ref)
    sign = jnp.where(row < 4, -1.0, 1.0)
    for i, value in enumerate(twiddle_sines(sub)):
        twiddle_ref[i] = value * sign

    def clear(s, carry):
        fill_ref[s] = 0
        return carry

    lax.fori_loop(0, owned, clear, 0)
    meta_copy.wait()
    recv_copy.wait()

    def gather(src, carry):
        moved = []
        for r in range(cap):
            count = meta_ref[src, 3, 2 * r].astype(jnp.int32)
            slot = meta_ref[src, 3, 2 * r + 1].astype(jnp.int32)
            p = fill_ref[slot]
            fill_ref[slot] = p + count
            shift = p % blk
            rows = (r % 2) * 4
            v = pltpu.roll(recv_ref[src, r], shift, 1)
            c = pltpu.roll(recv_ref[src, cap + r // 2], shift, 1)[rows : rows + 4]
            moved.append((slot * chunks + p // blk, lane < shift, v, c))
        for at, keep, v, c in moved:
            buf_v[at] = jnp.where(keep, buf_v[at], v)
            buf_c[at] = jnp.where(keep[0:4], buf_c[at], c)
            buf_v[at + 1] = v
            buf_c[at + 1] = c
        return carry

    lax.fori_loop(0, owners, gather, 0)

    unit = rowf * step
    first = row == 0
    dims = (((1,), (1,)), ((), ()))

    def chunk(slot, k):
        live = lane < fill_ref[slot] - k * blk
        at = slot * chunks + k
        vis = jnp.where(live, buf_v[at], 0.0)
        coords = jnp.where(live[0:4], buf_c[at], 0.0)
        u, v, w = coords[0:1], coords[1:2], coords[2:3]
        far = jnp.where(
            row < 2,
            u * jnp.where(row == 0, 8 * step, half * step),
            jnp.where(row < 4, v * jnp.where(row == 2, 8 * step, half * step), w * n_corner),
        )
        cos_f, sin_f = cos_sin_turns(far)
        cos_f, sin_f = [[x[i : i + 1] for i in range(5)] for x in (cos_f, sin_f)]

        def line(t, c8, s8):
            c, s = cos_sin_turns(t * unit)
            return [c, c * c8 - s * s8], [s, s * c8 + c * s8]

        cos_a, sin_a = line(u, cos_f[0], sin_f[0])
        cos_b, sin_b = line(v, cos_f[2], sin_f[2])
        for i in range(2):
            b_ref[0, 8 * i : 8 * i + 8] = cos_b[i]
            b_ref[1, 8 * i : 8 * i + 8] = sin_b[i]
        b_ref[0, half : half + 1] = cos_f[3]
        b_ref[1, half : half + 1] = sin_f[3]
        ca16, sa16 = cos_f[1], sin_f[1]

        for j in range(8):
            w_ref[0, 0, 8 * j : 8 * j + 8], w_ref[1, 0, 8 * j : 8 * j + 8] = cos_sin_turns(w * n_ref[j])
            both = cos_sin_turns(w * n_ref[8 + j])
            for i in range(2):
                w_ref[i, 1, 8 * j : 8 * j + 8] = both[i]
                w_ref[i, 2, 8 * j : 8 * j + 8] = both[i]
        diagonal = cos_sin_turns(w * n_ref[16])
        for j in range(8):
            for i in range(2):
                w_ref[i, 2, 9 * j : 9 * j + 1] = diagonal[i][j : j + 1]
        edge = [cos_sin_turns(w * n_ref[17 + i]) for i in range(2)]
        for i in range(2):
            cw, sw = edge[i]
            x16_ref[0, 8 * i : 8 * i + 8] = cw * ca16 + sw * sa16
            x16_ref[1, 8 * i : 8 * i + 8] = sw * ca16 - cw * sa16
        x16_ref[0, half : half + 1] = cos_f[4] * ca16 + sin_f[4] * sa16
        x16_ref[1, half : half + 1] = sin_f[4] * ca16 - cos_f[4] * sa16

        def plane(i, g):
            if g == half:
                return edge[0][i], edge[1][i]
            j = g % 8
            own, across = pl.ds(8 * j, 8), pl.ds(j, 8, stride=8)
            if g < 8:
                return jnp.where(row >= j, w_ref[i, 1, own], w_ref[i, 1, across]), w_ref[i, 0, own]
            return w_ref[i, 0, across], jnp.where(row <= j, w_ref[i, 2, own], w_ref[i, 2, across])

        turned = -sign * pltpu.roll(vis, 4, 0)
        at = pl.ds(pl.multiple_of(slot * 8, 8), 8)
        for g in range(half + 1):
            cw, sw = plane(0, g), plane(1, g)
            q1 = [cw[i] * cos_a[i] for i in range(2)]
            q2 = [sw[i] * cos_a[i] for i in range(2)]
            q3 = [cw[i] * sin_a[i] for i in range(2)]
            q4 = [sw[i] * sin_a[i] for i in range(2)]
            q3[0] = jnp.where(first, x16_ref[1, g : g + 1], q3[0])
            q4[0] = jnp.where(first, x16_ref[0, g : g + 1], q4[0])
            high, low = split(jnp.concatenate(q1 + q2 + q3 + q4, 0))
            straight, across = vis * b_ref[0, g : g + 1], turned * b_ref[1, g : g + 1]
            left_high, left_low = split(jnp.concatenate([straight + across, straight - across], 0))
            left = jnp.concatenate(
                [
                    jnp.concatenate([left_high, left_high], 1),
                    jnp.concatenate([left_low, left_low], 1),
                ],
                0,
            )
            out = lax.dot_general(
                left, jnp.concatenate([high, low], 1), dims, preferred_element_type=F32
            )
            if g < half:
                sums_ref[half + g, at] += out[0:8] + out[16:24]
            if g > 0:
                sums_ref[half - g, at] += out[8:16] + out[24:32]

    def one_slot(slot, carry):
        used = (fill_ref[slot] + (blk - 1)) // blk

        def step_chunk(k, c):
            chunk(slot, k)
            return c

        return lax.fori_loop(0, used, step_chunk, carry)

    lax.fori_loop(0, owned, one_slot, 0)

    def along_x(y, carry):
        left = jnp.concatenate(split(sums_ref[y]), 1)
        high, low = high_ref[y], low_ref[y]
        right = jnp.concatenate([high, high, low, jnp.zeros_like(low)], 0)
        z_ref[y] = jnp.dot(jnp.concatenate([left, left], 1), right, preferred_element_type=F32)
        return carry

    lax.fori_loop(0, sub, along_x, 0, unroll=2)

    together = math.gcd(owned, LANES // sub)

    def times(x, k, count):
        if k == 0:
            return x
        k = k * (sub // count)
        cosine = math.cos(2 * math.pi * k / sub)
        sine = twiddle_ref[min(k, sub // 2 - k) - 1]
        turned = sine * pltpu.roll(x, 4, 0)
        return -turned if k == sub // 4 else cosine * x - turned

    def place(group, carry):
        lines = []
        for y in range(sub):
            real, imag = None, None
            for i in range(together):
                at = pl.ds(pl.multiple_of((group * together + i) * 8, 8), 8)
                re, im = z_ref[y, at, 0:LANES], z_ref[y, at, LANES : 2 * LANES]
                if i == 0:
                    real, imag = re, im
                else:
                    real = real + pltpu.roll(re, i * sub, 1)
                    imag = imag + pltpu.roll(im, i * sub, 1)
            lines.append(real + sign * pltpu.roll(imag, 4, 0))
        lines = fourier(lines, times)
        for i in range(together):
            slot = group * together + i
            corner_row, corner_col = offset_ref[slot, 0], offset_ref[slot, 1]
            here = (lane >= corner_col) & (lane < corner_col + sub)
            turn = (corner_col + (LANES - i * sub)) % LANES
            for ky in range(sub):
                moved = jnp.where(here, pltpu.roll(lines[ky], turn, 1), 0.0)
                tile_ref[corner_row + ky] += moved
        return carry

    lax.fori_loop(0, owned // together, place, 0)

    rows = TILE // parts
    for p in range(parts):
        which = lax.rem(part_ref[0] + p, parts)
        outs[p][...] = tile_ref[pl.ds(which * rows, rows)]


def tile_parts(offsets, part, recv, high, low, cap, parts):
    owners, tiles, _, blk = recv.shape
    owned = offsets.shape[0]
    sub = high.shape[0]
    half = sub // 2
    chunks = owners * cap + 1
    smem = pl.BlockSpec(memory_space=pltpu.SMEM)
    vmem = pl.BlockSpec(memory_space=pltpu.VMEM)
    rows = TILE // parts
    return pl.pallas_call(
        functools.partial(tile_kernel, cap=cap, sub=sub, parts=parts, chunks=chunks),
        out_shape=[jax.ShapeDtypeStruct((rows, COMPS, TILE), F32)] * parts,
        in_specs=[smem, smem, pl.BlockSpec(memory_space=pl.ANY), vmem, vmem],
        out_specs=[vmem] * parts,
        scratch_shapes=[
            pltpu.SMEM((owners, 8, blk), F32),
            pltpu.SMEM((owned,), jnp.int32),
            pltpu.VMEM((owners, tiles, 8, blk), F32),
            pltpu.VMEM((half + 3, 8, blk), F32),
            pltpu.VMEM((owned * chunks + 1, 8, blk), F32),
            pltpu.VMEM((owned * chunks + 1, 4, blk), F32),
            pltpu.VMEM((2, half + 8, blk), F32),
            pltpu.VMEM((2, 3, 64, blk), F32),
            pltpu.VMEM((2, half + 8, blk), F32),
            pltpu.VMEM((sub, owned * 8, 4 * half), F32),
            pltpu.VMEM((sub, owned * 8, 2 * LANES), F32),
            pltpu.VMEM((TILE, COMPS, TILE), F32),
            pltpu.VMEM((sub // 4, 8, LANES), F32),
            pltpu.SemaphoreType.DMA((2,)),
        ],
        name="tile",
    )(offsets, part, recv, high, low)


def shards(
    visibility, uv_offset, w_offset, taper, row_count, block_owner, block_slot, subgrid_offset
):
    blocks_here, blk = visibility.shape[1], visibility.shape[3]
    owners = lax.axis_size("uv")
    parts = lax.axis_size("freq")
    cap = 2 * blocks_here // owners
    sent = pack(
        row_count[0],
        block_owner[0, :, 0],
        block_slot[0],
        visibility[0],
        uv_offset[0],
        w_offset[0],
        owners,
        cap,
    )
    recv = lax.all_to_all(sent, "uv", split_axis=0, concat_axis=0, tiled=True)
    high, low = tables(taper, blk)
    part = lax.axis_index("freq").astype(jnp.int32).reshape(1)
    pieces = tile_parts(subgrid_offset, part, recv, high, low, cap, parts)
    total = pieces[0]
    for s in range(1, parts):
        total = total + lax.ppermute(pieces[s], "freq", [(i, (i + s) % parts) for i in range(parts)])
    return total


def solution(mesh):
    placed = (
        P("freq", "uv", None, None),
        P("freq", "uv", None, None),
        P("freq", "uv", None),
        P(),
        P("freq", "uv"),
        P("freq", "uv", None),
        P("freq", "uv"),
        P("uv", None),
    )
    return jax.shard_map(
        shards, mesh=mesh, in_specs=placed, out_specs=P(("uv", "freq"), None, None), check_vma=False
    )
```

profile of v0, /device:TPU:1, one launch (start us, length us, event | category | flops | bytes accessed | tf_op | source)
XLA Modules:
  0.0 54.6 jit_solution(6176792232888373612)
XLA Ops:
  0.0 2.5 %pack.1 = f32[16,6,8,128]{3,2,1,0:T(8,128)} custom-call(s32[32]{0:T(128)} %bitcast.10, s32[32]{0:T(128)} %bitcast.11, s32[32]{0:T(128)} %bitcast.12, f32[32,8,128]{2,1,0:T(8,128)} %bitcast.7, f32[32,2,128]{2,1,0:T(2,128)} %bitcast.8, f32[32,128]{1,0:T(8,128)} %bitcast.9), custom_call_target="tpu_custom_call" | custom-call | tf_op jit(solution)/shard_map/pack/pallas_call | solution.py:94
  2.5 7.3 %all-to-all-start = ((f32[16,6,8,128]{3,2,1,0:T(8,128)}), f32[16,6,8,128]{3,2,1,0:T(8,128)S(1)}, u32[]{:S(2)}, u32[]{:S(2)}) async-start(f32[16,6,8,128]{3,2,1,0:T(8,128)} %pack.1), calls=%async_computation | async-start | bytes 786432 | tf_op jit(solution)/shard_map/all_to_all | solution.py:439
  9.8 0.0 copy-start.1
  9.8 0.7 %copy-done.1 = s32[16,2]{0,1:T(2,128)S(1)} copy-done((s32[16,2]{0,1:T(2,128)S(1)}, s32[16,2]{0,1:T(2,128)}, u32[]{:S(2)}) %copy-start.1) | copy-done | bytes 152
  10.5 0.7 %copy.11.offset_ref = s32[16,2]{1,0:T(8,128)} copy(s32[16,2]{0,1:T(2,128)S(1)} %copy-done.1) | data formatting | bytes 256 | tf_op args[7]
  11.2 3.1 %tables.1 = (bf16[32,64,256]{2,1,0:T(8,128)(2,1)}, bf16[32,64,256]{2,1,0:T(8,128)(2,1)}) custom-call(f32[32,32]{1,0:T(8,128)} %taper_ref.1, f32[2,64,256]{2,1,0:T(8,128)} %constant.8.clone.coef_ref, f32[2,64,32]{2,1,0:T(8,128)} %constant.9.clone.pick_ref), custom_call_target="tpu_custom_call" | custom-call | tf_op jit(solution)/shard_map/tables/pallas_call | solution.py:146
  14.3 7.4 %all-to-all-done.recv_hbm = f32[16,6,8,128]{3,2,1,0:T(8,128)S(1)} async-done(((f32[16,6,8,128]{3,2,1,0:T(8,128)}), f32[16,6,8,128]{3,2,1,0:T(8,128)S(1)}, u32[]{:S(2)}, u32[]{:S(2)}) %all-to-all-start) | async-done | bytes 393248 | tf_op jit(solution)/shard_map/all_to_all | solution.py:439
  21.7 0.0 copy-start
  21.7 0.7 %copy-done = f32[16,6,8,128]{3,2,1,0:T(8,128)} copy-done((f32[16,6,8,128]{3,2,1,0:T(8,128)}, f32[16,6,8,128]{3,2,1,0:T(8,128)S(1)}, u32[]{:S(2)}) %copy-start) | copy-done | bytes 393240
  22.4 25.0 %tile.1 = (f32[64,8,128]{2,1,0:T(8,128)}, f32[64,8,128]{2,1,0:T(8,128)}) custom-call(s32[16,2]{1,0:T(8,128)} %copy.11.offset_ref, s32[1]{0:T(128)} %bitcast.part_ref, f32[16,6,8,128]{3,2,1,0:T(8,128)} %copy-done, bf16[32,64,256]{2,1,0:T(8,128)(2,1)} %get-tuple-element.9.high_ref, bf16[32,64,256]{2,1,0:T(8,128)(2,1)} %get-tuple-element.10.low_ref), custom_call_target="tpu_custom_call" | custom-call | tf_op jit(solution)/shard_map/tile/pallas_call | solution.py:397
  47.4 1.3 %collective-permute-start = (f32[64,8,128]{2,1,0:T(8,128)}, f32[64,8,128]{2,1,0:T(8,128)S(1)}, u32[]{:S(2)}, u32[]{:S(2)}) collective-permute-start(f32[64,8,128]{2,1,0:T(8,128)} %get-tuple-element.12), channel_id=1, source_target_pairs={{0,1},{1,0},{2,3},{3,2},{4,5},{5,4},{6,7},{7,6},{8,9},{9,8},{10,11... | collective-permute-start | bytes 786440 | tf_op jit(solution)/shard_map/ppermute | solution.py:445
  48.7 4.2 %collective-permute-done = f32[64,8,128]{2,1,0:T(8,128)S(1)} collective-permute-done((f32[64,8,128]{2,1,0:T(8,128)}, f32[64,8,128]{2,1,0:T(8,128)S(1)}, u32[]{:S(2)}, u32[]{:S(2)}) %collective-permute-start) | collective-permute-done | bytes 262176 | tf_op jit(solution)/shard_map/ppermute | solution.py:445
  52.9 1.7 %add.3 = f32[64,8,128]{2,1,0:T(8,128)} add(f32[64,8,128]{2,1,0:T(8,128)} %get-tuple-element.11, f32[64,8,128]{2,1,0:T(8,128)S(1)} %collective-permute-done) | non-fusion elementwise | flops 65536 | bytes 786432 | tf_op jit(solution)/shard_map/add | solution.py:445
Async XLA Ops:
  2.5 19.2 %all-to-all-start = ((f32[16,6,8,128]{3,2,1,0:T(8,128)}), f32[16,6,8,128]{3,2,1,0:T(8,128)S(1)}, u32[]{:S(2)}, u32[]{:S(2)}) async-start(f32[16,6,8,128]{3,2,1,0:T(8,128)} %pack.1), calls=%async_computation | async-start | bytes 786432 | tf_op jit(solution)/shard_map/all_to_all | solution.py:439
  9.8 0.7 %copy-start.1 = (s32[16,2]{0,1:T(2,128)S(1)}, s32[16,2]{0,1:T(2,128)}, u32[]{:S(2)}) copy-start(s32[16,2]{0,1:T(2,128)} %param.17) | copy-start | bytes 388
  21.7 0.8 %copy-start = (f32[16,6,8,128]{3,2,1,0:T(8,128)}, f32[16,6,8,128]{3,2,1,0:T(8,128)S(1)}, u32[]{:S(2)}) copy-start(f32[16,6,8,128]{3,2,1,0:T(8,128)S(1)} %all-to-all-done.recv_hbm) | copy-start | bytes 1179652
  47.4 5.5 %collective-permute-start = (f32[64,8,128]{2,1,0:T(8,128)}, f32[64,8,128]{2,1,0:T(8,128)S(1)}, u32[]{:S(2)}, u32[]{:S(2)}) collective-permute-start(f32[64,8,128]{2,1,0:T(8,128)} %get-tuple-element.12), channel_id=1, source_target_pairs={{0,1},{1,0},{2,3},{3,2},{4,5},{5,4},{6,7},{7,6},{8,9},{9,8},{10,11... | collective-permute-start | bytes 786440 | tf_op jit(solution)/shard_map/ppermute | solution.py:445
where the time goes:
time: 55.7 us; the launch traced here: 54.6 us
  Pallas kernels  30.6 us (55%)
  waiting for transfers between devices  11.6 us (21%)
  starting transfers between devices  8.63 us (15%)
  local copies, waits for them, and re-layouts  2.1 us (4%)
  other arithmetic  1.69 us (3%)
    pallas_call x1, Pallas kernels, tile_parts(): pl.pallas_call(functools.partial(tile_kernel, cap=cap, sub=sub, parts=par...  25 us
    all_to_all x1, waiting for transfers between devices, shards(): recv = lax.all_to_all(sent, 'uv', split_axis=0, concat_axis=0, tiled=True)  7.37 us
    all_to_all x1, starting transfers between devices, shards(): recv = lax.all_to_all(sent, 'uv', split_axis=0, concat_axis=0, tiled=True)  7.34 us
    ppermute x1, waiting for transfers between devices, shards(): lax.ppermute(pieces[s], 'freq', [(i, (i + s) % parts) for i in range(part...  4.21 us
    pallas_call x1, Pallas kernels, tables(): pl.pallas_call(tables_kernel, out_shape=[shape, shape], in_specs=[vmem] *...  3.14 us
    pallas_call x1, Pallas kernels, pack(): pl.pallas_call(functools.partial(pack_kernel, cap=cap), out_shape=jax.Sha...  2.47 us
    unnamed x5, local copies, waits for them, and re-layouts  2.1 us
    add x1, other arithmetic, shards(): total + lax.ppermute(pieces[s], 'freq', [(i, (i + s) % parts) for i in ra...  1.69 us
  transfers between devices with their start and end apart: 2, of which 2 were waited for; matrix products, arithmetic and copies ran while one was open for 1% of the time, Pallas kernels for 6%

commit v1 on v0

v1 whole, which is shorter than its diff:
```python
import functools
import math

import jax
import jax.numpy as jnp
import numpy as np
from jax import lax
from jax.experimental import pallas as pl
from jax.experimental.pallas import tpu as pltpu
from jax.sharding import PartitionSpec as P

TILE = 128
LANES = 128
COMPS = 8
SIDES = 2
field_width = 0.5

F32 = jnp.float32
BF16 = jnp.bfloat16


def fit_even(function, degree):
    points = np.cos(np.pi * (np.arange(400) + 0.5) / 400) * 0.125 + 0.125
    fit = np.polynomial.chebyshev.Chebyshev.fit(points, function(np.sqrt(points)), degree, domain=[0, 0.25])
    return [float(c) for c in fit.convert(kind=np.polynomial.Polynomial).coef]


SIN_COEF = fit_even(lambda f: math.sqrt(2) * np.sin(np.pi * f) / f, 3)
COS_COEF = fit_even(lambda f: math.sqrt(2) * np.cos(np.pi * f), 4)


def cos_sin_turns(turns):
    frac = turns - jnp.round(turns)
    square = frac * frac
    cos_half = COS_COEF[-1] * square + COS_COEF[-2]
    sin_half = SIN_COEF[-1] * square + SIN_COEF[-2]
    for c in COS_COEF[-3::-1]:
        cos_half = cos_half * square + c
    for c in SIN_COEF[-3::-1]:
        sin_half = sin_half * square + c
    sin_half = sin_half * frac
    return 1.0 - sin_half * sin_half, sin_half * cos_half


def split(x):
    high = x.astype(BF16)
    return high, (x - high.astype(F32)).astype(BF16)


def iota(shape, axis):
    return lax.broadcasted_iota(jnp.int32, shape, axis)


def pack_kernel(count_ref, owner_ref, slot_ref, vis_ref, uv_ref, w_ref, out_ref, used_ref, *, cap):
    owners = out_ref.shape[0]
    blk = vis_ref.shape[2]
    blocks = vis_ref.shape[0]
    extra = out_ref.shape[1] - cap
    shape = (8, blk)
    row, lane = iota(shape, 0), iota(shape, 1)

    def clear(o, carry):
        used_ref[o] = 0
        for t in range(extra):
            out_ref[o, cap + t] = jnp.zeros(shape, F32)
        return carry

    lax.fori_loop(0, owners, clear, 0)

    def place(j, carry):
        o = owner_ref[j]
        r = used_ref[o]
        used_ref[o] = r + 1
        count = count_ref[j]
        out_ref[o, r] = vis_ref[j]
        u, v, w = uv_ref[j, 0:1, :], uv_ref[j, 1:2, :], w_ref[pl.ds(j, 1), :]
        part = row % 4
        coords = jnp.where(part == 0, u, jnp.where(part == 1, v, w))
        t = cap + r // 2
        mine = (row // 4 == r % 2) & (part < 3)
        out_ref[o, t] = jnp.where(mine, coords, out_ref[o, t])
        meta = jnp.where(lane == 2 * r, count.astype(F32), slot_ref[j].astype(F32))
        here = (row == 3) & (lane // 2 == r)
        out_ref[o, cap] = jnp.where(here, meta, out_ref[o, cap])
        return carry

    lax.fori_loop(0, blocks, place, 0)


def pack(counts, owner, slot, vis, uv, w, owners, cap):
    extra = (cap + 1) // 2
    blk = vis.shape[2]
    smem = pl.BlockSpec(memory_space=pltpu.SMEM)
    vmem = pl.BlockSpec(memory_space=pltpu.VMEM)
    return pl.pallas_call(
        functools.partial(pack_kernel, cap=cap),
        out_shape=jax.ShapeDtypeStruct((owners, cap + extra, 8, blk), F32),
        in_specs=[smem] * 3 + [vmem] * 3,
        out_specs=vmem,
        scratch_shapes=[pltpu.SMEM((owners,), jnp.int32)],
        name="pack",
    )(counts, owner, slot, vis, uv, w)


def transform_constants(sub, blk, pack):
    half = sub // 2
    scale = 1.0 / math.sqrt(blk) / sub
    k = np.arange(sub)
    both = np.zeros((2, 4, half, sub), np.complex128)
    pick = np.zeros((2, 4, half, sub), np.float32)
    for a in range(half):
        up = np.exp(-2j * np.pi * k * (half + a) / sub) * scale
        down = np.exp(-2j * np.pi * k * (half - a) / sub) * scale
        pick[0, :, a, half + a] = 1
        pick[1, :, a, half - a if a else 0] = 1
        if a == 0:
            both[0, 0, 0], both[0, 1, 0] = up, -1j * up
            both[1, 2, 0], both[1, 3, 0] = -1j * scale, scale
        else:
            both[0, :, a] = [up, -1j * up, -1j * up, -up]
            both[1, :, a] = [down, -1j * down, 1j * down, down]
    both = both.reshape(2, 4 * half, sub)
    coef = np.zeros((2, pack, 2, 4 * half, LANES), np.float32)
    for i in range(pack):
        coef[:, i, 0, :, i * sub : (i + 1) * sub] = both.real
        coef[:, i, 1, :, i * sub : (i + 1) * sub] = both.imag
    return coef, pick.reshape(2, 4 * half, sub)


def tables_kernel(taper_ref, coef_ref, pick_ref, high_ref, low_ref):
    sub = taper_ref.shape[0]
    pack, rows = coef_ref.shape[1], coef_ref.shape[3]
    dims = (((1,), (1,)), ((), ()))
    plus, minus = [
        lax.dot_general(pick_ref[i], taper_ref[...], dims, precision=lax.Precision.HIGHEST)
        for i in range(2)
    ]
    for y in range(sub):
        up = jnp.broadcast_to(plus[:, y : y + 1], (rows, LANES))
        down = jnp.broadcast_to(minus[:, y : y + 1], (rows, LANES))
        for i in range(pack):
            for part in range(2):
                at = (y, pl.ds(i * rows, rows), pl.ds(part * LANES, LANES))
                m = up * coef_ref[0, i, part] + down * coef_ref[1, i, part]
                high_ref[at], low_ref[at] = split(m)


def tables(taper, blk):
    sub = taper.shape[0]
    pack = LANES // (2 * sub)
    coef, pick = transform_constants(sub, blk, pack)
    vmem = pl.BlockSpec(memory_space=pltpu.VMEM)
    shape = jax.ShapeDtypeStruct((sub, LANES, 2 * LANES), BF16)
    return pl.pallas_call(
        tables_kernel,
        out_shape=[shape, shape],
        in_specs=[vmem] * 3,
        out_specs=[vmem] * 2,
        name="tables",
    )(taper, jnp.asarray(coef), jnp.asarray(pick))


def twiddle_sines(sub):
    return [math.sin(2 * math.pi * k / sub) for k in range(1, sub // 4 + 1)]


def fourier(values, times):
    count = len(values)
    if count == 1:
        return values
    even, odd = fourier(values[0::2], times), fourier(values[1::2], times)
    odd = [times(x, k, count) for k, x in enumerate(odd)]
    return [e + o for e, o in zip(even, odd)] + [e - o for e, o in zip(even, odd)]


def lane_sums_row(place, pack, stride):
    return lax.rem(place, pack) * stride + lax.div(place, pack) * 8


def tile_kernel(*refs, inside, cap, sub, parts, chunks):
    if inside:
        offset_ref, part_ref, kept_ref, kept_v, kept_c, high_hbm, low_hbm, base_ref, out_ref, *rest = refs
    else:
        offset_ref, part_ref, recv_hbm, high_hbm, low_hbm = refs[:5]
        outs = refs[5 : 5 + parts]
        kept_ref, kept_v, kept_c, *rest = refs[5 + parts :]
        meta_ref, order_ref, place_ref, fill_ref, at_ref, live_ref, to_ref, recv_ref, buf_v, buf_c, *rest = rest
        owners = recv_ref.shape[0]
    (
        n_ref, b_ref, w_ref, x16_ref, sums_ref, z_ref, lines_ref, tile_ref, twiddle_ref, high_ref, low_ref, sems,
    ) = rest
    owned = offset_ref.shape[0]
    blk = kept_v.shape[2]
    half = sub // 2
    pack = LANES // (2 * sub)
    stride = owned // pack * 8
    keep_rows = TILE // parts
    head = owned + 3
    shape = (8, blk)
    row, lane = iota(shape, 0), iota(shape, 1)
    blk_log = blk.bit_length() - 1
    assert half == 16 and blk == 1 << blk_log
    table_copies = [
        pltpu.make_async_copy(high_hbm, high_ref, sems.at[2]),
        pltpu.make_async_copy(low_hbm, low_ref, sems.at[3]),
    ]
    if not inside:
        meta_copy = pltpu.make_async_copy(recv_hbm.at[:, cap, 3], meta_ref, sems.at[0])
        recv_copy = pltpu.make_async_copy(recv_hbm, recv_ref, sems.at[1])
        meta_copy.start()
        recv_copy.start()
    for copy in table_copies:
        copy.start()

    first_row = part_ref[0] * keep_rows
    if inside:
        listed, count_all = kept_ref[0], kept_ref[1]
    else:

        def clear(s, carry):
            fill_ref[s] = 0
            order_ref[s] = 0
            kept_ref[2 + s] = 0
            return carry

        lax.fori_loop(0, owned + 1, clear, 0)

        def choose(s, n):
            corner = offset_ref[s, 0]
            within = (corner >= first_row) & (corner + sub <= first_row + keep_rows)
            place_ref[s] = jnp.where(within, owned - 1 - (s - n), n)
            order_ref[n] = s
            kept_ref[2 + s - n] = s
            return n + jnp.where(within, 0, 1)

        count_all = lax.fori_loop(0, owned, choose, 0)
    groups = lax.div(count_all + (pack - 1), pack)

    step = field_width / sub
    rowf = row.astype(F32)

    def n_of(y, x):
        s = (x * x + y * y) * (step * step)
        return s / (1.0 + jnp.sqrt(1.0 - s))

    for j in range(8):
        n_ref[j] = n_of(float(j), rowf + 8.0)
        shifted = jnp.where(row >= j, 0.0, 8.0)
        n_ref[8 + j] = n_of(float(j) + shifted, rowf + shifted)
    n_ref[16] = n_of(rowf + 8.0, rowf + 8.0)
    n_ref[17] = n_of(float(half), rowf)
    n_ref[18] = n_of(float(half), rowf + 8.0)
    s_corner = 2.0 * half * half * step * step
    n_corner = s_corner / (1.0 + math.sqrt(1.0 - s_corner))
    sign = jnp.where(row < 4, -1.0, 1.0)
    for i, value in enumerate(twiddle_sines(sub)):
        twiddle_ref[i] = value * sign
    if inside:
        tile_ref[0:keep_rows] = base_ref[...]
        tile_ref[keep_rows:] = jnp.zeros((sub, COMPS, TILE), F32)
    else:
        tile_ref[...] = jnp.zeros_like(tile_ref)

    def clear_sums(group, carry):
        for i in range(pack):
            at = pl.ds(pl.multiple_of(i * stride + group * 8, 8), 8)
            for y in range(sub):
                sums_ref[y, at] = jnp.zeros((8, 4 * half), F32)
        return carry

    lax.fori_loop(0, groups, clear_sums, 0)
    if not inside:
        meta_copy.wait()
        recv_copy.wait()

        def gather(src, carry):
            moved = []
            for r in range(cap):
                count = meta_ref[src, 2 * r].astype(jnp.int32)
                place = place_ref[meta_ref[src, 2 * r + 1].astype(jnp.int32)]
                p = fill_ref[place]
                fill_ref[place] = p + count
                shift = p & (blk - 1)
                rows = (r % 2) * 4
                v = pltpu.roll(recv_ref[src, r], shift, 1)
                c = pltpu.roll(recv_ref[src, cap + r // 2], shift, 1)[rows : rows + 4]
                moved.append((place * chunks + lax.shift_right_logical(p, blk_log), lane < shift, v, c))
            for at, keep, v, c in moved:
                buf_v[at] = jnp.where(keep, buf_v[at], v)
                buf_c[at] = jnp.where(keep[0:4], buf_c[at], c)
                buf_v[at + 1] = v
                buf_c[at + 1] = c
            return carry

        lax.fori_loop(0, owners, gather, 0, unroll=2)

        def list_chunks(place, n):
            fill = fill_ref[place]
            to = lane_sums_row(place, pack, stride)

            def one(k, n):
                at_ref[n] = place * chunks + k
                live_ref[n] = fill - k * blk
                to_ref[n] = to
                return n + 1

            return lax.fori_loop(0, lax.shift_right_logical(fill + (blk - 1), blk_log), one, n)

        listed = lax.fori_loop(0, count_all, list_chunks, 0)
        for i in range(SIDES - 1):
            for ref in (at_ref, live_ref, to_ref):
                ref[listed + i] = 0

        def keep_chunks(i, n):
            place = owned - 1 - i
            fill = fill_ref[place]
            to = lane_sums_row(i, pack, stride)

            def one(k, n):
                live = lane < fill - k * blk
                kept_v[n] = jnp.where(live, buf_v[place * chunks + k], 0.0)
                kept_c[n] = jnp.where(live[0:4], buf_c[place * chunks + k], 0.0)
                kept_ref[head + n] = to
                return n + 1

            return lax.fori_loop(0, lax.shift_right_logical(fill + (blk - 1), blk_log), one, n)

        kept = lax.fori_loop(0, owned - count_all, keep_chunks, 0)
        for i in range(SIDES - 1):
            kept_v[kept + i] = jnp.zeros(shape, F32)
            kept_c[kept + i] = jnp.zeros((4, blk), F32)
            kept_ref[head + kept + i] = 0
        kept_ref[0] = kept
        kept_ref[1] = owned - count_all

    unit = rowf * step
    first = row == 0
    dims = (((1,), (1,)), ((), ()))

    def chunk(number, side):
        if inside:
            vis, coords, to = kept_v[number], kept_c[number], kept_ref[head + number]
        else:
            at, to = at_ref[number], to_ref[number]
            live = lane < live_ref[number]
            vis = jnp.where(live, buf_v[at], 0.0)
            coords = jnp.where(live[0:4], buf_c[at], 0.0)
        u, v, w = coords[0:1], coords[1:2], coords[2:3]
        far = jnp.where(
            row < 2,
            u * jnp.where(row == 0, 8 * step, half * step),
            jnp.where(row < 4, v * jnp.where(row == 2, 8 * step, half * step), w * n_corner),
        )
        cos_f, sin_f = cos_sin_turns(far)
        cos_f, sin_f = [[x[i : i + 1] for i in range(5)] for x in (cos_f, sin_f)]

        def line(t, c8, s8):
            c, s = cos_sin_turns(t * unit)
            return [c, c * c8 - s * s8], [s, s * c8 + c * s8]

        cos_a, sin_a = line(u, cos_f[0], sin_f[0])
        cos_b, sin_b = line(v, cos_f[2], sin_f[2])
        for i in range(2):
            b_ref[side, 0, 8 * i : 8 * i + 8] = cos_b[i]
            b_ref[side, 1, 8 * i : 8 * i + 8] = sin_b[i]
        b_ref[side, 0, half : half + 1] = cos_f[3]
        b_ref[side, 1, half : half + 1] = sin_f[3]
        ca16, sa16 = cos_f[1], sin_f[1]

        for j in range(8):
            both = cos_sin_turns(w * n_ref[8 + j])
            for i in range(2):
                w_ref[side, i, 1, 8 * j : 8 * j + 8] = both[i]
                w_ref[side, i, 2, 8 * j : 8 * j + 8] = both[i]
        diagonal = cos_sin_turns(w * n_ref[16])
        for j in range(8):
            for i in range(2):
                w_ref[side, i, 2, 9 * j : 9 * j + 1] = diagonal[i][j : j + 1]
        edge = [cos_sin_turns(w * n_ref[17 + i]) for i in range(2)]
        for i in range(2):
            cw, sw = edge[i]
            x16_ref[side, 0, 8 * i : 8 * i + 8] = cw * ca16 + sw * sa16
            x16_ref[side, 1, 8 * i : 8 * i + 8] = sw * ca16 - cw * sa16
        x16_ref[side, 0, half : half + 1] = cos_f[4] * ca16 + sin_f[4] * sa16
        x16_ref[side, 1, half : half + 1] = sin_f[4] * ca16 - cos_f[4] * sa16
        turned = -sign * pltpu.roll(vis, 4, 0)
        to = pl.ds(pl.multiple_of(to, 8), 8)

        def add(g, cw, sw):
            q1 = [cw[i] * cos_a[i] for i in range(2)]
            q2 = [sw[i] * cos_a[i] for i in range(2)]
            q3 = [cw[i] * sin_a[i] for i in range(2)]
            q4 = [sw[i] * sin_a[i] for i in range(2)]
            q3[0] = jnp.where(first, x16_ref[side, 1, g : g + 1], q3[0])
            q4[0] = jnp.where(first, x16_ref[side, 0, g : g + 1], q4[0])
            right = jnp.concatenate(split(jnp.concatenate(q1 + q2 + q3 + q4, 0)), 1)
            straight, across = vis * b_ref[side, 0, g : g + 1], turned * b_ref[side, 1, g : g + 1]
            left = jnp.concatenate(split(jnp.concatenate([straight + across, straight - across], 0)), 0)
            out = lax.dot_general(
                jnp.concatenate([left, left], 1), right, dims, preferred_element_type=F32
            )
            if g < half:
                sums_ref[half + g, to] += out[0:8] + out[16:24]
            if g > 0:
                sums_ref[half - g, to] += out[8:16] + out[24:32]

        add(half, [edge[i][0] for i in range(2)], [edge[i][1] for i in range(2)])
        for j in range(8):
            own, across = pl.ds(8 * j, 8), pl.ds(j, 8, stride=8)
            far_pair = cos_sin_turns(w * n_ref[j])
            pairs = []
            for i in range(2):
                w_ref[side, i, 0, 8 * j : 8 * j + 8] = far_pair[i]
                near = jnp.where(row >= j, w_ref[side, i, 1, own], w_ref[side, i, 1, across])
                pairs.append([near, far_pair[i]])
            add(j, *pairs)
        for j in range(8):
            own, across = pl.ds(8 * j, 8), pl.ds(j, 8, stride=8)
            pairs = []
            for i in range(2):
                far_one = jnp.where(row <= j, w_ref[side, i, 2, own], w_ref[side, i, 2, across])
                pairs.append([w_ref[side, i, 0, across], far_one])
            add(8 + j, *pairs)

    def some_chunks(i, carry):
        for side in range(SIDES):
            chunk(SIDES * i + side, side)
        return carry

    lax.fori_loop(0, lax.div(listed + (SIDES - 1), SIDES), some_chunks, 0)

    for copy in table_copies:
        copy.wait()

    def transform_x(used):
        def along_x(y, carry):
            sums = [sums_ref[y, i * stride : i * stride + used] for i in range(pack)]
            high, low = split(jnp.concatenate(sums, 1))
            right = jnp.concatenate([high_ref[y], high_ref[y]], 0)
            z_ref[y, 0:used] = jnp.dot(
                jnp.concatenate([high, low], 1), right, preferred_element_type=F32
            ) + jnp.dot(high, low_ref[y], preferred_element_type=F32)
            return carry

        lax.fori_loop(0, sub, along_x, 0, unroll=8)

    if inside:
        few = stride // 2

        @pl.when(groups * 8 <= few)
        def _():
            transform_x(few)

        @pl.when(groups * 8 > few)
        def _():
            transform_x(stride)
    else:
        transform_x(stride)

    def times(x, k, count):
        if k == 0:
            return x
        k = k * (sub // count)
        cosine = math.cos(2 * math.pi * k / sub)
        sine = twiddle_ref[min(k, sub // 2 - k) - 1]
        turned = sine * pltpu.roll(x, 4, 0)
        return -turned if k == sub // 4 else cosine * x - turned

    top_row = tile_ref.shape[0] - sub

    def put(group):
        def one(i, ky, turn, here, corner_row):
            moved = jnp.where(here, pltpu.roll(lines_ref[ky], turn, 1), 0.0)
            tile_ref[corner_row + ky] += moved

        steps = []
        for i in range(pack):
            slot = (kept_ref if inside else order_ref)[group * pack + i + (2 if inside else 0)]
            corner_row, corner_col = offset_ref[slot, 0], offset_ref[slot, 1]
            if inside:
                corner_row = jnp.clip(corner_row - first_row, 0, top_row)
            here = (lane >= corner_col) & (lane < corner_col + sub)
            turn = (corner_col + (LANES - i * sub)) & (LANES - 1)
            steps += [functools.partial(one, i, ky, turn, here, corner_row) for ky in range(sub)]
        return steps

    def place(group, carry):
        steps = put(jnp.maximum(group - 1, 0))
        at = pl.ds(pl.multiple_of(group * 8, 8), 8)
        lines = []
        for y in range(sub):
            for step_of in steps[y * pack : (y + 1) * pack]:
                step_of()
            real, imag = z_ref[y, at, 0:LANES], z_ref[y, at, LANES : 2 * LANES]
            lines.append(real + sign * pltpu.roll(imag, 4, 0))
        lines = fourier(lines, times)
        for ky in range(sub):
            lines_ref[ky] = lines[ky]
        return carry

    lines_ref[...] = jnp.zeros_like(lines_ref)
    lax.fori_loop(0, groups, place, 0)
    for step_of in put(jnp.maximum(groups - 1, 0)):
        step_of()

    if inside:
        out_ref[...] = tile_ref[0:keep_rows]
    else:
        for p in range(parts):
            which = lax.rem(part_ref[0] + p, parts)
            outs[p][...] = tile_ref[pl.ds(which * keep_rows, keep_rows)]


def tile_rows(offsets, part, given, high, low, cap, parts, base=None):
    inside = base is not None
    owned = offsets.shape[0]
    sub = high.shape[0]
    half = sub // 2
    blk = LANES
    smem = pl.BlockSpec(memory_space=pltpu.SMEM)
    vmem = pl.BlockSpec(memory_space=pltpu.VMEM)
    anywhere = pl.BlockSpec(memory_space=pl.ANY)
    rows = TILE // parts
    shape = jax.ShapeDtypeStruct((rows, COMPS, TILE), F32)
    scratch, chunks = [], None
    if inside:
        operands = [*given, high, low, base]
        in_specs = [smem, vmem, vmem, anywhere, anywhere, vmem]
        out_shape, out_specs = shape, vmem
    else:
        owners, tiles, _, blk = given.shape
        chunks = owners * cap + 1
        most = owners * cap + SIDES
        index = pltpu.SMEM((owned + 1,), jnp.int32)
        listing = pltpu.SMEM((most,), jnp.int32)
        operands = [given, high, low]
        in_specs = [anywhere] * 3
        out_shape = [shape] * parts + [
            jax.ShapeDtypeStruct((owned + 3 + most,), jnp.int32),
            jax.ShapeDtypeStruct((most, 8, blk), F32),
            jax.ShapeDtypeStruct((most, 4, blk), F32),
        ]
        out_specs = [vmem] * parts + [smem, vmem, vmem]
        scratch = [
            pltpu.SMEM((owners, blk), F32),
            index,
            index,
            index,
            listing,
            listing,
            listing,
            pltpu.VMEM((owners, tiles, 8, blk), F32),
            pltpu.VMEM((owned * chunks + 1, 8, blk), F32),
            pltpu.VMEM((owned * chunks + 1, 4, blk), F32),
        ]
    return pl.pallas_call(
        functools.partial(tile_kernel, inside=inside, cap=cap, sub=sub, parts=parts, chunks=chunks),
        out_shape=out_shape,
        in_specs=[smem, smem, *in_specs],
        out_specs=out_specs,
        scratch_shapes=scratch
        + [
            pltpu.VMEM((half + 3, 8, blk), F32),
            pltpu.VMEM((SIDES, 2, half + 8, blk), F32),
            pltpu.VMEM((SIDES, 2, 3, 64, blk), F32),
            pltpu.VMEM((SIDES, 2, half + 8, blk), F32),
            pltpu.VMEM((sub, owned * 8, 4 * half), F32),
            pltpu.VMEM((sub, owned * 2 * sub * 8 // LANES, 2 * LANES), F32),
            pltpu.VMEM((sub, 8, LANES), F32),
            pltpu.VMEM((rows + sub if inside else TILE, COMPS, TILE), F32),
            pltpu.VMEM((sub // 4, 8, LANES), F32),
            pltpu.VMEM(high.shape, BF16),
            pltpu.VMEM(low.shape, BF16),
            pltpu.SemaphoreType.DMA((4,)),
        ],
        name="inner" if inside else "tile",
    )(offsets, part, *operands)


def shards(
    visibility, uv_offset, w_offset, taper, row_count, block_owner, block_slot, subgrid_offset
):
    blocks_here, blk = visibility.shape[1], visibility.shape[3]
    owners = lax.axis_size("uv")
    parts = lax.axis_size("freq")
    cap = 2 * blocks_here // owners
    sent = pack(
        row_count[0],
        block_owner[0, :, 0],
        block_slot[0],
        visibility[0],
        uv_offset[0],
        w_offset[0],
        owners,
        cap,
    )
    recv = lax.all_to_all(sent, "uv", split_axis=0, concat_axis=0, tiled=True)
    high, low = tables(taper, blk)
    part = lax.axis_index("freq").astype(jnp.int32).reshape(1)
    *pieces, kept, kept_v, kept_c = tile_rows(subgrid_offset, part, recv, high, low, cap, parts)
    moved = [
        lax.ppermute(pieces[s], "freq", [(i, (i + s) % parts) for i in range(parts)])
        for s in range(1, parts)
    ]
    total = tile_rows(
        subgrid_offset, part, (kept, kept_v, kept_c), high, low, cap, parts, pieces[0]
    )
    for piece in moved:
        total = total + piece
    return total


def solution(mesh):
    placed = (
        P("freq", "uv", None, None),
        P("freq", "uv", None, None),
        P("freq", "uv", None),
        P(),
        P("freq", "uv"),
        P("freq", "uv", None),
        P("freq", "uv"),
        P("uv", None),
    )
    return jax.shard_map(
        shards, mesh=mesh, in_specs=placed, out_specs=P(("uv", "freq"), None, None), check_vma=False
    )
```

time: 55.7 us -> 46.6 us (0.84)
  the two profiles are of different devices: /device:TPU:1 before, /device:TPU:15 now
where the time goes in v1:
time: 46.6 us; the launch traced here: 45.9 us
  Pallas kernels  29.4 us (63%)
  starting transfers between devices  7.58 us (16%)
  waiting for transfers between devices  5.12 us (11%)
  local copies, waits for them, and re-layouts  2.09 us (4%)
  other arithmetic  1.68 us (4%)
    pallas_call x2, Pallas kernels, tile_rows(): pl.pallas_call(functools.partial(tile_kernel, inside=inside, cap=cap, sub...  22.7 us
    all_to_all x1, starting transfers between devices, shards(): recv = lax.all_to_all(sent, 'uv', split_axis=0, concat_axis=0, tiled=True)  6.52 us
    all_to_all x1, waiting for transfers between devices, shards(): recv = lax.all_to_all(sent, 'uv', split_axis=0, concat_axis=0, tiled=True)  5.12 us
    pallas_call x1, Pallas kernels, tables(): pl.pallas_call(tables_kernel, out_shape=[shape, shape], in_specs=[vmem] *...  4.3 us
    pallas_call x1, Pallas kernels, pack(): pl.pallas_call(functools.partial(pack_kernel, cap=cap), out_shape=jax.Sha...  2.46 us
    unnamed x3, local copies, waits for them, and re-layouts  2.09 us
    add x1, other arithmetic, shards(): total = total + piece  1.68 us
    ppermute x1, starting transfers between devices, shards(): lax.ppermute(pieces[s], 'freq', [(i, (i + s) % parts) for i in range(part...  1.07 us
  transfers between devices with their start and end apart: 2, of which 1 were waited for; matrix products, arithmetic and copies ran while one was open for 3% of the time, Pallas kernels for 28%

profile of v1, /device:TPU:15, one launch (start us, length us, event | category | flops | bytes accessed | tf_op | source)
XLA Modules:
  0.0 45.9 jit_solution(2280498953689349892)
XLA Ops:
  0.0 2.5 %pack.1 = f32[16,6,8,128]{3,2,1,0:T(8,128)} custom-call(s32[32]{0:T(128)} %bitcast.10, s32[32]{0:T(128)} %bitcast.11, s32[32]{0:T(128)} %bitcast.12, f32[32,8,128]{2,1,0:T(8,128)} %bitcast.7, f32[32,2,128]{2,1,0:T(2,128)} %bitcast.8, f32[32,128]{1,0:T(8,128)} %bitcast.9), custom_call_target="tpu_custom_call" | custom-call | tf_op jit(solution)/shard_map/pack/pallas_call | solution.py:95
  2.5 6.5 %all-to-all-start = ((f32[16,6,8,128]{3,2,1,0:T(8,128)}), f32[16,6,8,128]{3,2,1,0:T(8,128)S(1)}, u32[]{:S(2)}, u32[]{:S(2)}) async-start(f32[16,6,8,128]{3,2,1,0:T(8,128)} %pack.1), calls=%async_computation | async-start | bytes 786432 | tf_op jit(solution)/shard_map/all_to_all | solution.py:597
  9.0 1.3 %copy.12.refs_0_ = s32[16,2]{1,0:T(8,128)} copy(s32[16,2]{0,1:T(2,128)} %param.17) | data formatting | bytes 256 | tf_op args[7]
  10.3 4.3 %tables.1 = (bf16[32,128,256]{2,1,0:T(8,128)(2,1)}, bf16[32,128,256]{2,1,0:T(8,128)(2,1)}) custom-call(f32[32,32]{1,0:T(8,128)} %taper_ref.1, f32[2,2,2,64,128]{4,3,2,1,0:T(8,128)} %constant.8.clone.coef_ref, f32[2,64,32]{2,1,0:T(8,128)} %constant.9.clone.pick_ref), custom_call_target="tpu_custom_call" | custom-call | tf_op jit(solution)/shard_map/tables/pallas_call | solution.py:154
  14.6 5.1 %all-to-all-done.refs_2_ = f32[16,6,8,128]{3,2,1,0:T(8,128)S(1)} async-done(((f32[16,6,8,128]{3,2,1,0:T(8,128)}), f32[16,6,8,128]{3,2,1,0:T(8,128)S(1)}, u32[]{:S(2)}, u32[]{:S(2)}) %all-to-all-start) | async-done | bytes 393248 | tf_op jit(solution)/shard_map/all_to_all | solution.py:597
  19.7 0.0 copy-start
  19.7 0.7 %copy-done = f32[16,6,8,128]{3,2,1,0:T(8,128)} copy-done((f32[16,6,8,128]{3,2,1,0:T(8,128)}, f32[16,6,8,128]{3,2,1,0:T(8,128)S(1)}, u32[]{:S(2)}) %copy-start) | copy-done | bytes 393240
  20.5 14.2 %tile.1 = (f32[64,8,128]{2,1,0:T(8,128)}, f32[64,8,128]{2,1,0:T(8,128)}, s32[85]{0:T(128)}, f32[66,8,128]{2,1,0:T(8,128)}, f32[66,4,128]{2,1,0:T(4,128)}) custom-call(s32[16,2]{1,0:T(8,128)} %copy.12.refs_0_, s32[1]{0:T(128)} %bitcast.refs_1_, f32[16,6,8,128]{3,2,1,0:T(8,128)} %copy-done, bf16[32,128,256]{2,1,0:T(8,128)(2,1)} %get-tuple-element.12.refs_3_.refs_5_, ...), custom_call_target="tpu_custom_call" | custom-call | tf_op jit(solution)/shard_map/tile/pallas_call | solution.py:556
  34.7 1.1 %collective-permute-start = (f32[64,8,128]{2,1,0:T(8,128)}, f32[64,8,128]{2,1,0:T(8,128)S(1)}, u32[]{:S(2)}, u32[]{:S(2)}) collective-permute-start(f32[64,8,128]{2,1,0:T(8,128)} %get-tuple-element.18), channel_id=1, source_target_pairs={{0,1},{1,0},{2,3},{3,2},{4,5},{5,4},{6,7},{7,6},{8,9},{9,8},{10,11... | collective-permute-start | bytes 786440 | tf_op jit(solution)/shard_map/ppermute | solution.py:602
  35.7 8.5 %inner.1 = f32[64,8,128]{2,1,0:T(8,128)} custom-call(s32[16,2]{1,0:T(8,128)} %copy.12.refs_0_, s32[1]{0:T(128)} %bitcast.refs_1_, s32[85]{0:T(128)} %get-tuple-element.14.refs_2_, f32[66,8,128]{2,1,0:T(8,128)} %get-tuple-element.15.refs_3_, f32[66,4,128]{2,1,0:T(4,128)} %get-tuple-element.16.refs_4_, ...), custom_call_target="tpu_custom_call" | custom-call | tf_op jit(solution)/shard_map/inner/pallas_call | solution.py:556
  44.2 0.0 collective-permute-done
  44.2 1.7 %add.3 = f32[64,8,128]{2,1,0:T(8,128)} add(f32[64,8,128]{2,1,0:T(8,128)} %inner.1, f32[64,8,128]{2,1,0:T(8,128)S(1)} %collective-permute-done) | non-fusion elementwise | flops 65536 | bytes 786432 | tf_op jit(solution)/shard_map/add | solution.py:609
Async XLA Ops:
  2.5 17.3 %all-to-all-start = ((f32[16,6,8,128]{3,2,1,0:T(8,128)}), f32[16,6,8,128]{3,2,1,0:T(8,128)S(1)}, u32[]{:S(2)}, u32[]{:S(2)}) async-start(f32[16,6,8,128]{3,2,1,0:T(8,128)} %pack.1), calls=%async_computation | async-start | bytes 786432 | tf_op jit(solution)/shard_map/all_to_all | solution.py:597
  19.7 0.7 %copy-start = (f32[16,6,8,128]{3,2,1,0:T(8,128)}, f32[16,6,8,128]{3,2,1,0:T(8,128)S(1)}, u32[]{:S(2)}) copy-start(f32[16,6,8,128]{3,2,1,0:T(8,128)S(1)} %all-to-all-done.refs_2_) | copy-start | bytes 1179652
  34.7 9.6 %collective-permute-start = (f32[64,8,128]{2,1,0:T(8,128)}, f32[64,8,128]{2,1,0:T(8,128)S(1)}, u32[]{:S(2)}, u32[]{:S(2)}) collective-permute-start(f32[64,8,128]{2,1,0:T(8,128)} %get-tuple-element.18), channel_id=1, source_target_pairs={{0,1},{1,0},{2,3},{3,2},{4,5},{5,4},{6,7},{7,6},{8,9},{9,8},{10,11... | collective-permute-start | bytes 786440 | tf_op jit(solution)/shard_map/ppermute | solution.py:602

commit v2 on v1

--- a/solution.py
+++ b/solution.py
@@ -45,6 +45,10 @@
 def split(x):
     high = x.astype(BF16)
     return high, (x - high.astype(F32)).astype(BF16)
+
+
+def in_vmem(x):
+    return pltpu.with_memory_space_constraint(x, pltpu.VMEM)
 
 
 def iota(shape, axis):
@@ -120,16 +124,17 @@
             both[0, :, a] = [up, -1j * up, -1j * up, -up]
             both[1, :, a] = [down, -1j * down, 1j * down, down]
     both = both.reshape(2, 4 * half, sub)
-    coef = np.zeros((2, pack, 2, 4 * half, LANES), np.float32)
+    coef = np.zeros((2, pack, 4 * half, LANES), np.float32)
     for i in range(pack):
-        coef[:, i, 0, :, i * sub : (i + 1) * sub] = both.real
-        coef[:, i, 1, :, i * sub : (i + 1) * sub] = both.imag
+        for part, values in enumerate((both.real, both.imag)):
+            at = (part * pack + i) * sub
+            coef[:, i, :, at : at + sub] = values
     return coef, pick.reshape(2, 4 * half, sub)
 
 
-def tables_kernel(taper_ref, coef_ref, pick_ref, high_ref, low_ref):
+def tables_kernel(taper_ref, coef_ref, pick_ref, table_ref):
     sub = taper_ref.shape[0]
-    pack, rows = coef_ref.shape[1], coef_ref.shape[3]
+    pack, rows = coef_ref.shape[1], coef_ref.shape[2]
     dims = (((1,), (1,)), ((), ()))
     plus, minus = [
         lax.dot_general(pick_ref[i], taper_ref[...], dims, precision=lax.Precision.HIGHEST)
@@ -139,10 +144,8 @@
         up = jnp.broadcast_to(plus[:, y : y + 1], (rows, LANES))
         down = jnp.broadcast_to(minus[:, y : y + 1], (rows, LANES))
         for i in range(pack):
-            for part in range(2):
-                at = (y, pl.ds(i * rows, rows), pl.ds(part * LANES, LANES))
-                m = up * coef_ref[0, i, part] + down * coef_ref[1, i, part]
-                high_ref[at], low_ref[at] = split(m)
+            at = pl.ds(i * rows, rows)
+            table_ref[0, y, at], table_ref[1, y, at] = split(up * coef_ref[0, i] + down * coef_ref[1, i])
 
 
 def tables(taper, blk):
@@ -150,13 +153,13 @@
     pack = LANES // (2 * sub)
     coef, pick = transform_constants(sub, blk, pack)
     vmem = pl.BlockSpec(memory_space=pltpu.VMEM)
-    shape = jax.ShapeDtypeStruct((sub, LANES, 2 * LANES), BF16)
     return pl.pallas_call(
         tables_kernel,
-        out_shape=[shape, shape],
+        out_shape=jax.ShapeDtypeStruct((2, sub, LANES, LANES), BF16),
         in_specs=[vmem] * 3,
-        out_specs=[vmem] * 2,
+        out_specs=vmem,
         name="tables",
+        compiler_params=pltpu.CompilerParams(vmem_limit_bytes=16 << 20),
     )(taper, jnp.asarray(coef), jnp.asarray(pick))
 
 
@@ -179,15 +182,15 @@
 
 def tile_kernel(*refs, inside, cap, sub, parts, chunks):
     if inside:
-        offset_ref, part_ref, kept_ref, kept_v, kept_c, high_hbm, low_hbm, base_ref, out_ref, *rest = refs
+        offset_ref, part_ref, kept_ref, kept_v, kept_c, table_ref, base_ref, out_ref, *rest = refs
     else:
-        offset_ref, part_ref, recv_hbm, high_hbm, low_hbm = refs[:5]
-        outs = refs[5 : 5 + parts]
-        kept_ref, kept_v, kept_c, *rest = refs[5 + parts :]
-        meta_ref, order_ref, place_ref, fill_ref, at_ref, live_ref, to_ref, recv_ref, buf_v, buf_c, *rest = rest
+        offset_ref, part_ref, recv_ref, table_ref = refs[:4]
+        outs = refs[4 : 4 + parts]
+        kept_ref, kept_v, kept_c, *rest = refs[4 + parts :]
+        meta_ref, order_ref, place_ref, fill_ref, at_ref, live_ref, to_ref, buf_v, buf_c, sem, *rest = rest
         owners = recv_ref.shape[0]
     (
-        n_ref, b_ref, w_ref, x16_ref, sums_ref, z_ref, lines_ref, tile_ref, twiddle_ref, high_ref, low_ref, sems,
+        n_ref, b_ref, w_ref, x16_ref, sums_ref, z_ref, lines_ref, tile_ref, twiddle_ref,
     ) = rest
     owned = offset_ref.shape[0]
     blk = kept_v.shape[2]
@@ -200,17 +203,9 @@
     row, lane = iota(shape, 0), iota(shape, 1)
     blk_log = blk.bit_length() - 1
     assert half == 16 and blk == 1 << blk_log
-    table_copies = [
-        pltpu.make_async_copy(high_hbm, high_ref, sems.at[2]),
-        pltpu.make_async_copy(low_hbm, low_ref, sems.at[3]),
-    ]
     if not inside:
-        meta_copy = pltpu.make_async_copy(recv_hbm.at[:, cap, 3], meta_ref, sems.at[0])
-        recv_copy = pltpu.make_async_copy(recv_hbm, recv_ref, sems.at[1])
+        meta_copy = pltpu.make_async_copy(recv_ref.at[:, cap, 3], meta_ref, sem)
         meta_copy.start()
-        recv_copy.start()
-    for copy in table_copies:
-        copy.start()
 
     first_row = part_ref[0] * keep_rows
     if inside:
@@ -271,7 +266,6 @@
     lax.fori_loop(0, groups, clear_sums, 0)
     if not inside:
         meta_copy.wait()
-        recv_copy.wait()
 
         def gather(src, carry):
             moved = []
@@ -429,17 +423,14 @@
 
     lax.fori_loop(0, lax.div(listed + (SIDES - 1), SIDES), some_chunks, 0)
 
-    for copy in table_copies:
-        copy.wait()
-
     def transform_x(used):
         def along_x(y, carry):
             sums = [sums_ref[y, i * stride : i * stride + used] for i in range(pack)]
             high, low = split(jnp.concatenate(sums, 1))
-            right = jnp.concatenate([high_ref[y], high_ref[y]], 0)
+            right = jnp.concatenate([table_ref[0, y], table_ref[0, y]], 0)
             z_ref[y, 0:used] = jnp.dot(
                 jnp.concatenate([high, low], 1), right, preferred_element_type=F32
-            ) + jnp.dot(high, low_ref[y], preferred_element_type=F32)
+            ) + jnp.dot(high, table_ref[1, y], preferred_element_type=F32)
             return carry
 
         lax.fori_loop(0, sub, along_x, 0, unroll=8)
@@ -491,8 +482,9 @@
         for y in range(sub):
             for step_of in steps[y * pack : (y + 1) * pack]:
                 step_of()
-            real, imag = z_ref[y, at, 0:LANES], z_ref[y, at, LANES : 2 * LANES]
-            lines.append(real + sign * pltpu.roll(imag, 4, 0))
+            pair = z_ref[y, at]
+            imag = pltpu.roll(pair, LANES // 2, 1)
+            lines.append(pair + sign * pltpu.roll(imag, 4, 0))
         lines = fourier(lines, times)
         for ky in range(sub):
             lines_ref[ky] = lines[ky]
@@ -511,30 +503,29 @@
             outs[p][...] = tile_ref[pl.ds(which * keep_rows, keep_rows)]
 
 
-def tile_rows(offsets, part, given, high, low, cap, parts, base=None):
+def tile_rows(offsets, part, given, table, cap, parts, base=None):
     inside = base is not None
     owned = offsets.shape[0]
-    sub = high.shape[0]
+    sub = table.shape[1]
     half = sub // 2
     blk = LANES
     smem = pl.BlockSpec(memory_space=pltpu.SMEM)
     vmem = pl.BlockSpec(memory_space=pltpu.VMEM)
-    anywhere = pl.BlockSpec(memory_space=pl.ANY)
     rows = TILE // parts
     shape = jax.ShapeDtypeStruct((rows, COMPS, TILE), F32)
     scratch, chunks = [], None
     if inside:
-        operands = [*given, high, low, base]
-        in_specs = [smem, vmem, vmem, anywhere, anywhere, vmem]
+        operands = [*given, table, base]
+        in_specs = [smem] + [vmem] * 4
         out_shape, out_specs = shape, vmem
     else:
-        owners, tiles, _, blk = given.shape
+        owners, _, _, blk = given.shape
         chunks = owners * cap + 1
         most = owners * cap + SIDES
         index = pltpu.SMEM((owned + 1,), jnp.int32)
         listing = pltpu.SMEM((most,), jnp.int32)
-        operands = [given, high, low]
-        in_specs = [anywhere] * 3
+        operands = [given, table]
+        in_specs = [vmem] * 2
         out_shape = [shape] * parts + [
             jax.ShapeDtypeStruct((owned + 3 + most,), jnp.int32),
             jax.ShapeDtypeStruct((most, 8, blk), F32),
@@ -549,9 +540,9 @@
             listing,
             listing,
             listing,
-            pltpu.VMEM((owners, tiles, 8, blk), F32),
             pltpu.VMEM((owned * chunks + 1, 8, blk), F32),
             pltpu.VMEM((owned * chunks + 1, 4, blk), F32),
+            pltpu.SemaphoreType.DMA,
         ]
     return pl.pallas_call(
         functools.partial(tile_kernel, inside=inside, cap=cap, sub=sub, parts=parts, chunks=chunks),
@@ -565,15 +556,13 @@
             pltpu.VMEM((SIDES, 2, 3, 64, blk), F32),
             pltpu.VMEM((SIDES, 2, half + 8, blk), F32),
             pltpu.VMEM((sub, owned * 8, 4 * half), F32),
-            pltpu.VMEM((sub, owned * 2 * sub * 8 // LANES, 2 * LANES), F32),
+            pltpu.VMEM((sub, owned * 2 * sub * 8 // LANES, LANES), F32),
             pltpu.VMEM((sub, 8, LANES), F32),
             pltpu.VMEM((rows + sub if inside else TILE, COMPS, TILE), F32),
             pltpu.VMEM((sub // 4, 8, LANES), F32),
-            pltpu.VMEM(high.shape, BF16),
-            pltpu.VMEM(low.shape, BF16),
-            pltpu.SemaphoreType.DMA((4,)),
         ],
         name="inner" if inside else "tile",
+        compiler_params=pltpu.CompilerParams(vmem_limit_bytes=20 << 20),
     )(offsets, part, *operands)
 
 
@@ -595,15 +584,22 @@
         cap,
     )
     recv = lax.all_to_all(sent, "uv", split_axis=0, concat_axis=0, tiled=True)
-    high, low = tables(taper, blk)
+    recv = in_vmem(recv)
+    table = in_vmem(tables(taper, blk))
     part = lax.axis_index("freq").astype(jnp.int32).reshape(1)
-    *pieces, kept, kept_v, kept_c = tile_rows(subgrid_offset, part, recv, high, low, cap, parts)
+    *pieces, kept, kept_v, kept_c = tile_rows(subgrid_offset, part, recv, table, cap, parts)
     moved = [
         lax.ppermute(pieces[s], "freq", [(i, (i + s) % parts) for i in range(parts)])
         for s in range(1, parts)
     ]
     total = tile_rows(
-        subgrid_offset, part, (kept, kept_v, kept_c), high, low, cap, parts, pieces[0]
+        subgrid_offset,
+        part,
+        (kept, in_vmem(kept_v), in_vmem(kept_c)),
+        table,
+        cap,
+        parts,
+        in_vmem(pieces[0]),
     )
     for piece in moved:
         total = total + piece

time: 46.6 us -> 43.6 us (0.936)
  the two profiles are of different devices: /device:TPU:15 before, /device:TPU:7 now
where the time goes in v2:
time: 43.6 us; the launch traced here: 44.1 us
  Pallas kernels  25.3 us (58%)
  starting transfers between devices  7.75 us (18%)
  waiting for transfers between devices  7.04 us (16%)
  local copies, waits for them, and re-layouts  3.21 us (7%)
  other arithmetic  0.74 us (2%)
    pallas_call x2, Pallas kernels, tile_rows(): pl.pallas_call(functools.partial(tile_kernel, inside=inside, cap=cap, sub...  22 us
    all_to_all x1, waiting for transfers between devices, shards(): recv = lax.all_to_all(sent, 'uv', split_axis=0, concat_axis=0, tiled=True)  7.04 us
    all_to_all x1, starting transfers between devices, shards(): recv = lax.all_to_all(sent, 'uv', split_axis=0, concat_axis=0, tiled=True)  6.63 us
    unnamed x7, local copies, waits for them, and re-layouts  3.21 us
    pallas_call x1, Pallas kernels, pack(): pl.pallas_call(functools.partial(pack_kernel, cap=cap), out_shape=jax.Sha...  2.48 us
    ppermute x1, starting transfers between devices, shards(): lax.ppermute(pieces[s], 'freq', [(i, (i + s) % parts) for i in range(part...  1.11 us
  transfers between devices with their start and end apart: 2, of which 1 were waited for; matrix products, arithmetic and copies ran while one was open for 2% of the time, Pallas kernels for 22%

profile of v2, /device:TPU:7, one launch (start us, length us, event | category | flops | bytes accessed | tf_op | source)
XLA Modules:
  0.0 44.1 jit_solution(13729078476758357312)
XLA Ops:
  0.0 2.5 %pack.1 = f32[16,6,8,128]{3,2,1,0:T(8,128)} custom-call(s32[32]{0:T(128)} %bitcast.10, s32[32]{0:T(128)} %bitcast.11, s32[32]{0:T(128)} %bitcast.12, f32[32,8,128]{2,1,0:T(8,128)} %bitcast.7, f32[32,2,128]{2,1,0:T(2,128)} %bitcast.8, f32[32,128]{1,0:T(8,128)} %bitcast.9), custom_call_target="tpu_custom_call" | custom-call | tf_op jit(solution)/shard_map/pack/pallas_call | solution.py:99
  2.5 6.6 %all-to-all-start = ((f32[16,6,8,128]{3,2,1,0:T(8,128)}), f32[16,6,8,128]{3,2,1,0:T(8,128)S(1)}, u32[]{:S(2)}, u32[]{:S(2)}) async-start(f32[16,6,8,128]{3,2,1,0:T(8,128)} %pack.1), calls=%async_computation | async-start | bytes 786432 | tf_op jit(solution)/shard_map/all_to_all | solution.py:586
  9.1 0.8 %copy.12.refs_0_ = s32[16,2]{1,0:T(8,128)S(1)} copy(s32[16,2]{0,1:T(2,128)} %param.17) | data formatting | bytes 256 | tf_op args[7]
  9.9 0.0 copy-start
  9.9 0.9 %copy-done = f32[2,2,64,128]{3,2,1,0:T(8,128)S(1)} copy-done((f32[2,2,64,128]{3,2,1,0:T(8,128)S(1)}, f32[2,2,64,128]{3,2,1,0:T(8,128)}, u32[]{:S(2)}) %copy-start) | copy-done | bytes 131096
  10.8 0.0 copy-start.1
  10.8 0.8 %copy-done.1 = f32[2,64,32]{2,1,0:T(8,128)S(1)} copy-done((f32[2,64,32]{2,1,0:T(8,128)S(1)}, f32[2,64,32]{2,1,0:T(8,128)}, u32[]{:S(2)}) %copy-start.1) | copy-done | bytes 16408
  11.6 0.0 copy-start.2
  11.6 0.7 %copy-done.2 = f32[32,32]{1,0:T(8,128)S(1)} copy-done((f32[32,32]{1,0:T(8,128)S(1)}, f32[32,32]{1,0:T(8,128)}, u32[]{:S(2)}) %copy-start.2) | copy-done | bytes 4120
  12.3 0.9 %tables.1.refs_3_.refs_5_ = bf16[2,32,128,128]{3,2,1,0:T(8,128)(2,1)S(1)} custom-call(f32[32,32]{1,0:T(8,128)S(1)} %copy-done.2, f32[2,2,64,128]{3,2,1,0:T(8,128)S(1)} %copy-done, f32[2,64,32]{2,1,0:T(8,128)S(1)} %copy-done.1), custom_call_target="tpu_custom_call" | custom-call | tf_op jit(solution)/shard_map/tables/pallas_call | solution.py:156
  13.2 7.0 %all-to-all-done.refs_2_ = f32[16,6,8,128]{3,2,1,0:T(8,128)S(1)} async-done(((f32[16,6,8,128]{3,2,1,0:T(8,128)}), f32[16,6,8,128]{3,2,1,0:T(8,128)S(1)}, u32[]{:S(2)}, u32[]{:S(2)}) %all-to-all-start) | async-done | bytes 393248 | tf_op jit(solution)/shard_map/all_to_all | solution.py:586
  20.2 13.0 %tile.1 = (f32[64,8,128]{2,1,0:T(8,128)S(1)}, f32[64,8,128]{2,1,0:T(8,128)S(1)}, s32[85]{0:T(128)S(1)}, f32[66,8,128]{2,1,0:T(8,128)S(1)}, f32[66,4,128]{2,1,0:T(4,128)S(1)}) custom-call(s32[16,2]{1,0:T(8,128)S(1)} %copy.12.refs_0_, s32[1]{0:T(128)} %bitcast.refs_1_, f32[16,6,8,128]{3,2,1,0:T(8,128)S(1)} %all-to-all-done.refs_2_, ...), custom_call_target="tpu_custom_call" | custom-call | tf_op jit(solution)/shard_map/tile/pallas_call | solution.py:547
  33.2 1.1 %collective-permute-start = (f32[64,8,128]{2,1,0:T(8,128)S(1)}, f32[64,8,128]{2,1,0:T(8,128)S(1)}, u32[]{:S(2)}, u32[]{:S(2)}) collective-permute-start(f32[64,8,128]{2,1,0:T(8,128)S(1)} %get-tuple-element.14), channel_id=1, source_target_pairs={{0,1},{1,0},{2,3},{3,2},{4,5},{5,4},{6,7},{7,6},{8,9},{9,8},{10,11... | collective-permute-start | bytes 786440 | tf_op jit(solution)/shard_map/ppermute | solution.py:592
  34.3 9.0 %inner.1 = f32[64,8,128]{2,1,0:T(8,128)S(1)} custom-call(s32[16,2]{1,0:T(8,128)S(1)} %copy.12.refs_0_, s32[1]{0:T(128)} %bitcast.refs_1_, s32[85]{0:T(128)S(1)} %get-tuple-element.10.refs_2_, f32[66,8,128]{2,1,0:T(8,128)S(1)} %get-tuple-element.11.refs_3_, f32[66,4,128]{2,1,0:T(4,128)S(1)} %get-tuple-element.12.refs_4_, ...), custom_call_target="tpu_custom_call" | custom-call | tf_op jit(solution)/shard_map/inner/pallas_call | solution.py:547
  43.3 0.0 collective-permute-done
  43.3 0.7 %add.3 = f32[64,8,128]{2,1,0:T(8,128)} add(f32[64,8,128]{2,1,0:T(8,128)S(1)} %inner.1, f32[64,8,128]{2,1,0:T(8,128)S(1)} %collective-permute-done) | non-fusion elementwise | flops 65536 | bytes 786432 | tf_op jit(solution)/shard_map/add | solution.py:605
Async XLA Ops:
  2.5 17.8 %all-to-all-start = ((f32[16,6,8,128]{3,2,1,0:T(8,128)}), f32[16,6,8,128]{3,2,1,0:T(8,128)S(1)}, u32[]{:S(2)}, u32[]{:S(2)}) async-start(f32[16,6,8,128]{3,2,1,0:T(8,128)} %pack.1), calls=%async_computation | async-start | bytes 786432 | tf_op jit(solution)/shard_map/all_to_all | solution.py:586
  9.9 0.9 %copy-start = (f32[2,2,64,128]{3,2,1,0:T(8,128)S(1)}, f32[2,2,64,128]{3,2,1,0:T(8,128)}, u32[]{:S(2)}) copy-start(f32[2,2,64,128]{3,2,1,0:T(8,128)} %constant.8.clone.coef_ref) | copy-start | bytes 393220
  10.8 0.8 %copy-start.1 = (f32[2,64,32]{2,1,0:T(8,128)S(1)}, f32[2,64,32]{2,1,0:T(8,128)}, u32[]{:S(2)}) copy-start(f32[2,64,32]{2,1,0:T(8,128)} %constant.9.clone.pick_ref) | copy-start | bytes 49156
  11.6 0.7 %copy-start.2 = (f32[32,32]{1,0:T(8,128)S(1)}, f32[32,32]{1,0:T(8,128)}, u32[]{:S(2)}) copy-start(f32[32,32]{1,0:T(8,128)} %taper_ref.1) | copy-start | bytes 12292
  33.2 10.1 %collective-permute-start = (f32[64,8,128]{2,1,0:T(8,128)S(1)}, f32[64,8,128]{2,1,0:T(8,128)S(1)}, u32[]{:S(2)}, u32[]{:S(2)}) collective-permute-start(f32[64,8,128]{2,1,0:T(8,128)S(1)} %get-tuple-element.14), channel_id=1, source_target_pairs={{0,1},{1,0},{2,3},{3,2},{4,5},{5,4},{6,7},{7,6},{8,9},{9,8},{10,11... | collective-permute-start | bytes 786440 | tf_op jit(solution)/shard_map/ppermute | solution.py:592
